TPU v7x, 32 devices: a whole 2x2x4 slice. The times are simulated.
32 devices in a mesh: parts: 32 (over z, y, x, core).
Axes of the slice: x: 2, y: 2, z: 4, core: 2. Of those that a mesh axis runs over, the one named last changes fastest.
Arguments:
- basis: float32 [16, 32768], P(None, 'parts'), may hold values from -8000 to 8000, as said below
- k_tiles: float32 [256, 5, 128, 128], P('parts'), may hold values from -3 to 11, as said below
- m_tiles: float32 [256, 5, 128, 128], P('parts'), may hold values from -2 to 4, as said below
- tile_part: int32 [256, 5], P('parts'), may hold values from 0 to 31, as said below
- tile_slot: int32 [256, 5], P('parts'), may hold values from 0 to 7, as said below
- iface_rows: int32 [64], P('parts'), may hold values from 0 to 7
Outputs:
- corrections: float32 [16, 32768], P(None, 'parts')
- theta: float32 [16], replicated
Inputs may be any that keep to these rules, and one draw needn't show every extreme that they name: `basis`: the rows form a full-rank set. `k_tiles`: block 0 of every row tile has a positive diagonal well above its other entries. `m_tiles`: block 0 of every row tile has a positive diagonal. `tile_part`: block 0 of a row tile lies in its own partition; every other block lies in its own partition, in the partition 1 away on either side, or in the partition 16 away, counted modulo the number of partitions. `tile_slot`: where the block lies in the own partition this is a row tile of it (for block 0 the row tile itself); elsewhere an interface slot below 2.
All inputs are finite; a program needn't handle non-finite values.
Results may differ from a plain program's by a relative error of at most 0.0003.
Values sent between devices are 32-bit elements; how exact they have to be, the bound alone decides.
No kernel may reach another device: no remote copies, remote signals or barrier semaphores. Data moves between devices by JAX's collectives and lax.ppermute only.
A program may use at most 64 MiB of HBM per device.

v0:
```python
import jax
import jax.numpy as jnp
from jax import lax
from jax.sharding import PartitionSpec as P

STEPS = 4
relax = 0.4


def shifted(value, axis, steps):
    count = lax.axis_size(axis)
    pairs = [(source, (source + steps) % count) for source in range(count)]
    return lax.ppermute(value, axis, pairs)


def product(left, right):
    return jnp.dot(left, right, precision=lax.Precision.HIGHEST, preferred_element_type=jnp.float32)


def inverse_lower(chol):
    eye = jnp.eye(chol.shape[0], dtype=chol.dtype)
    return jax.scipy.linalg.solve_triangular(chol, eye, lower=True)


def shards(basis, k_tiles, m_tiles, tile_part, tile_slot, iface_rows):
    pairs = basis.shape[0]
    tiles = k_tiles.shape[0]
    width = k_tiles.shape[2]
    count = iface_rows.shape[0]
    parts = lax.axis_size("parts")
    me = lax.axis_index("parts")
    scale = 1.0 / (basis.shape[1] * parts)
    far_step = parts // 2
    neighbours = (1, -1, far_step, -far_step)
    direction = jnp.full_like(tile_part, 3)
    for number in (2, 1, 0):
        target = (me + neighbours[number] + parts) % parts
        direction = jnp.where(tile_part == target, number, direction)
    remote = tiles + direction * count + tile_slot
    columns = jnp.where(tile_part == me, tile_slot, remote)

    def apply_pair(vectors):
        blocks = vectors.reshape(pairs, tiles, width)
        outgoing = jnp.take(blocks, iface_rows, axis=1)
        received = []
        for offset in neighbours:
            received.append(shifted(outgoing, "parts", -offset))
        incoming = jnp.concatenate(received, axis=1)
        sources = jnp.concatenate([blocks, incoming], axis=1)
        picked = jnp.take(sources, columns, axis=1)
        stiff = jnp.einsum("ptbc,tbrc->ptr", picked, k_tiles, precision=lax.Precision.HIGHEST)
        mass = jnp.einsum("ptbc,tbrc->ptr", picked, m_tiles, precision=lax.Precision.HIGHEST)
        return (stiff.reshape(pairs, -1), mass.reshape(pairs, -1))

    gram = lax.psum(product(basis, basis.T) * scale, "parts")
    inv_v = inverse_lower(jnp.linalg.cholesky(gram))
    ortho = product(inv_v, basis)
    k_ortho, m_ortho = apply_pair(ortho)
    mass_gram, stiff_cross = lax.psum(
        (product(m_ortho, m_ortho.T) * scale, product(m_ortho, k_ortho.T) * scale), "parts"
    )
    chol_b = jnp.linalg.cholesky(mass_gram)
    inv_b = inverse_lower(chol_b)
    test_basis = product(inv_b, m_ortho)
    projected_k = product(inv_b, stiff_cross)
    theta = jnp.diagonal(projected_k) / jnp.diagonal(chol_b)
    resid = k_ortho - theta[:, None] * m_ortho
    diag_k = jnp.diagonal(k_tiles[:, 0], axis1=1, axis2=2).reshape(-1)
    correct = -relax * resid / diag_k
    for step in range(STEPS):
        right = lax.psum(product(correct, ortho.T) * scale, "parts")
        moved = correct - product(right, ortho)
        k_moved, m_moved = apply_pair(moved)
        image = k_moved - theta[:, None] * m_moved
        left = lax.psum(product(image, test_basis.T) * scale, "parts")
        image = image - product(left, test_basis)
        correct = correct - relax * (resid + image) / diag_k
    final = lax.psum(product(correct, ortho.T) * scale, "parts")
    correct = correct - product(final, ortho)
    return (correct, theta)


def solution(mesh):
    placed = (
        P(None, "parts"),
        P("parts", None, None, None),
        P("parts", None, None, None),
        P("parts", None),
        P("parts", None),
        P("parts"),
    )
    return jax.shard_map(
        shards, mesh=mesh, in_specs=placed, out_specs=(P(None, "parts"), P()), check_vma=False
    )
```

profile of v0, /device:TPU:0, one launch (start us, length us, event | category | flops | bytes accessed | tf_op | source)
XLA Modules:
  0.0 536.0 jit_solution(4131112549924731336)
XLA Ops:
  0.6 0.8 compare_select_fusion.1
  2.1 1.1 convolution_multiply_fusion.9
  3.2 42.1 %psum.84 = f32[16,16]{0,1:T(8,128)S(1)} all-reduce(f32[16,16]{0,1:T(8,128)S(1)} %convolution_multiply_fusion.9), channel_id=1, replica_groups=mesh['parts'=32] {'parts'}, use_global_device_ids=true, to_apply=%region_0.1 | all-reduce | flops 256 | bytes 2048 | tf_op jit(solution)/shard_map/psum | solution.py:55
  45.3 1.5 cholesky.44
  48.1 1.2 custom-call.12
  49.6 1.0 fusion.99
  51.3 2.5 collective-permute-start
  53.8 0.8 collective-permute-start.2
  54.6 0.7 compare_and_fusion
  55.4 1.1 slice.11
  56.5 4.6 copy.65
  61.1 1.8 gather_fusion.2
  63.6 4.3 fusion.32
  68.0 2.6 fusion.30
  71.0 40.2 %all-reduce = (f32[16,16]{0,1:T(8,128)S(1)}, f32[16,16]{0,1:T(8,128)S(1)}) all-reduce(f32[16,16]{0,1:T(8,128)S(1)} %fusion.21, f32[16,16]{0,1:T(8,128)S(1)} %fusion.20), channel_id=1, replica_groups=mesh['parts'=32] {'parts'}, use_global_device_ids=true, to_apply=%region_3.8 | all-reduce | flops 512 | bytes 4096 | tf_op jit(solution)/shard_map/psum | solution.py:59
  111.3 1.5 cholesky.55
  114.1 1.2 custom-call.13
  115.9 0.7 gather_fusion
  117.5 39.9 %psum.87 = f32[16,16]{0,1:T(8,128)S(1)} all-reduce(f32[16,16]{0,1:T(8,128)S(1)} %convolution_multiply_fusion.8), channel_id=1, replica_groups=mesh['parts'=32] {'parts'}, use_global_device_ids=true, to_apply=%region_5.10 | all-reduce | flops 256 | bytes 2048 | tf_op jit(solution)/shard_map/psum | solution.py:71
  158.3 2.2 collective-permute-start.3
  160.7 1.8 collective-permute-start.5
  162.5 5.0 collective-permute-done.4
  168.1 2.6 convolution_bitcast_fusion.6
  170.8 2.6 convolution_bitcast_fusion.7
  173.7 36.9 %psum.88 = f32[16,16]{0,1:T(8,128)S(1)} all-reduce(f32[16,16]{0,1:T(8,128)S(1)} %convolution_multiply_fusion.7), channel_id=1, replica_groups=mesh['parts'=32] {'parts'}, use_global_device_ids=true, to_apply=%region_6.11 | all-reduce | flops 256 | bytes 2048 | tf_op jit(solution)/shard_map/psum | solution.py:75
  211.0 41.0 %psum.89 = f32[16,16]{0,1:T(8,128)S(1)} all-reduce(f32[16,16]{0,1:T(8,128)S(1)} %convolution_multiply_fusion.6), channel_id=1, replica_groups=mesh['parts'=32] {'parts'}, use_global_device_ids=true, to_apply=%region_7.12 | all-reduce | flops 256 | bytes 2048 | tf_op jit(solution)/shard_map/psum | solution.py:71
  252.9 1.8 collective-permute-start.6
  255.2 1.0 collective-permute-done.6
  256.2 5.3 collective-permute-done.7
  262.2 2.6 convolution_bitcast_fusion.4
  264.8 2.6 convolution_bitcast_fusion.5
  267.7 37.4 %psum.90 = f32[16,16]{0,1:T(8,128)S(1)} all-reduce(f32[16,16]{0,1:T(8,128)S(1)} %convolution_multiply_fusion.5), channel_id=1, replica_groups=mesh['parts'=32] {'parts'}, use_global_device_ids=true, to_apply=%region_8.13 | all-reduce | flops 256 | bytes 2048 | tf_op jit(solution)/shard_map/psum | solution.py:75
  305.5 41.0 %psum.91 = f32[16,16]{0,1:T(8,128)S(1)} all-reduce(f32[16,16]{0,1:T(8,128)S(1)} %convolution_multiply_fusion.4), channel_id=1, replica_groups=mesh['parts'=32] {'parts'}, use_global_device_ids=true, to_apply=%region_9.14 | all-reduce | flops 256 | bytes 2048 | tf_op jit(solution)/shard_map/psum | solution.py:71
  347.5 1.9 collective-permute-start.9
  349.5 1.4 collective-permute-done.9
  350.8 5.3 collective-permute-done.10
  356.8 2.6 convolution_bitcast_fusion.2
  359.4 2.6 convolution_bitcast_fusion.3
  362.3 36.9 %psum.92 = f32[16,16]{0,1:T(8,128)S(1)} all-reduce(f32[16,16]{0,1:T(8,128)S(1)} %convolution_multiply_fusion.3), channel_id=1, replica_groups=mesh['parts'=32] {'parts'}, use_global_device_ids=true, to_apply=%region_10.15 | all-reduce | flops 256 | bytes 2048 | tf_op jit(solution)/shard_map/psum | solution.py:75
  399.7 41.0 %psum.93 = f32[16,16]{0,1:T(8,128)S(1)} all-reduce(f32[16,16]{0,1:T(8,128)S(1)} %convolution_multiply_fusion.2), channel_id=1, replica_groups=mesh['parts'=32] {'parts'}, use_global_device_ids=true, to_apply=%region_11.16 | all-reduce | flops 256 | bytes 2048 | tf_op jit(solution)/shard_map/psum | solution.py:71
  441.6 1.9 collective-permute-start.12
  443.7 1.2 collective-permute-done.12
  444.9 5.5 %collective-permute-done.13 = f32[16,2,128]{2,0,1:T(8,128)S(1)} collective-permute-done((f32[16,2,128]{2,0,1:T(8,128)S(1)}, f32[16,2,128]{2,0,1:T(8,128)S(1)}, u32[]{:S(2)}, u32[]{:S(2)}) %collective-permute-start.13) | collective-permute-done | bytes 16416 | tf_op jit(solution)/shard_map/ppermute | solution.py:13
  451.0 2.6 convolution_bitcast_fusion
  453.7 2.6 convolution_bitcast_fusion.1
  456.6 36.9 %psum.94 = f32[16,16]{0,1:T(8,128)S(1)} all-reduce(f32[16,16]{0,1:T(8,128)S(1)} %convolution_multiply_fusion.1), channel_id=1, replica_groups=mesh['parts'=32] {'parts'}, use_global_device_ids=true, to_apply=%region_12.17 | all-reduce | flops 256 | bytes 2048 | tf_op jit(solution)/shard_map/psum | solution.py:75
  493.9 41.0 %psum.95 = f32[16,16]{0,1:T(8,128)S(1)} all-reduce(f32[16,16]{0,1:T(8,128)S(1)} %convolution_multiply_fusion), channel_id=1, replica_groups=mesh['parts'=32] {'parts'}, use_global_device_ids=true, to_apply=%region_13.18 | all-reduce | flops 256 | bytes 2048 | tf_op jit(solution)/shard_map/psum | solution.py:78
  535.0 0.9 convolution_subtract_fusion
  (116 shorter events, 16.9 us)
Async XLA Ops:
  0.6 67.4 %copy-start = (f32[8,5,128,128]{3,2,1,0:T(8,128)S(1)}, f32[8,5,128,128]{3,2,1,0:T(8,128)}, u32[]{:S(2)}) copy-start(f32[8,5,128,128]{3,2,1,0:T(8,128)} %param.15) | copy-start | bytes 7864324
  51.3 11.7 %collective-permute-start = (f32[16,2,128]{2,0,1:T(8,128)S(1)}, f32[16,2,128]{2,0,1:T(8,128)S(1)}, u32[]{:S(2)}, u32[]{:S(2)}) collective-permute-start(f32[16,2,128]{2,0,1:T(8,128)S(1)} %select_bitcast_fusion.4), channel_id=1, source_target_pairs={{0,31},{1,0},{2,1},{3,2},{4,3},{5,4},{6,5},{7,6},{8,7},{9,8},{10,9... | collective-permute-start | bytes 49160 | tf_op jit(solution)/shard_map/ppermute | solution.py:13
  53.8 9.2 %collective-permute-start.1 = (f32[16,2,128]{2,0,1:T(8,128)S(1)}, f32[16,2,128]{2,0,1:T(8,128)S(1)}, u32[]{:S(2)}, u32[]{:S(2)}) collective-permute-start(f32[16,2,128]{2,0,1:T(8,128)S(1)} %select_bitcast_fusion.4), channel_id=1, source_target_pairs={{0,1},{1,2},{2,3},{3,4},{4,5},{5,6},{6,7},{7,8},{8,9},{9,10},{10,1... | collective-permute-start | bytes 49160 | tf_op jit(solution)/shard_map/ppermute | solution.py:13
  53.8 9.2 %collective-permute-start.2 = (f32[16,2,128]{2,0,1:T(8,128)S(1)}, f32[16,2,128]{2,0,1:T(8,128)S(1)}, u32[]{:S(2)}, u32[]{:S(2)}) collective-permute-start(f32[16,2,128]{2,0,1:T(8,128)S(1)} %select_bitcast_fusion.4), channel_id=1, source_target_pairs={{0,16},{1,17},{2,18},{3,19},{4,20},{5,21},{6,22},{7,23},{8,24},{9,... | collective-permute-start | bytes 49160 | tf_op jit(solution)/shard_map/ppermute | solution.py:13
  117.2 376.2 %copy-start.5 = (f32[16]{0:T(128)}, f32[16]{0:T(128)S(1)}, u32[]{:S(2)}) copy-start(f32[16]{0:T(128)S(1)} %div.47) | copy-start | bytes 196
  158.3 4.2 collective-permute-start.3
  160.5 7.0 %collective-permute-start.4 = (f32[16,2,128]{2,0,1:T(8,128)S(1)}, f32[16,2,128]{2,0,1:T(8,128)S(1)}, u32[]{:S(2)}, u32[]{:S(2)}) collective-permute-start(f32[16,2,128]{2,0,1:T(8,128)S(1)} %select_bitcast_fusion.3), channel_id=1, source_target_pairs={{0,1},{1,2},{2,3},{3,4},{4,5},{5,6},{6,7},{7,8},{8,9},{9,10},{10,1... | collective-permute-start | bytes 49160 | tf_op jit(solution)/shard_map/ppermute | solution.py:13
  160.7 6.8 %collective-permute-start.5 = (f32[16,2,128]{2,0,1:T(8,128)S(1)}, f32[16,2,128]{2,0,1:T(8,128)S(1)}, u32[]{:S(2)}, u32[]{:S(2)}) collective-permute-start(f32[16,2,128]{2,0,1:T(8,128)S(1)} %select_bitcast_fusion.3), channel_id=1, source_target_pairs={{0,16},{1,17},{2,18},{3,19},{4,20},{5,21},{6,22},{7,23},{8,24},{9,... | collective-permute-start | bytes 49160 | tf_op jit(solution)/shard_map/ppermute | solution.py:13
  168.1 2.6 copy-start.1
  252.9 3.3 collective-permute-start.6
  254.8 6.8 %collective-permute-start.7 = (f32[16,2,128]{2,0,1:T(8,128)S(1)}, f32[16,2,128]{2,0,1:T(8,128)S(1)}, u32[]{:S(2)}, u32[]{:S(2)}) collective-permute-start(f32[16,2,128]{2,0,1:T(8,128)S(1)} %select_bitcast_fusion.2), channel_id=1, source_target_pairs={{0,1},{1,2},{2,3},{3,4},{4,5},{5,6},{6,7},{7,8},{8,9},{9,10},{10,1... | collective-permute-start | bytes 49160 | tf_op jit(solution)/shard_map/ppermute | solution.py:13
  254.8 6.8 %collective-permute-start.8 = (f32[16,2,128]{2,0,1:T(8,128)S(1)}, f32[16,2,128]{2,0,1:T(8,128)S(1)}, u32[]{:S(2)}, u32[]{:S(2)}) collective-permute-start(f32[16,2,128]{2,0,1:T(8,128)S(1)} %select_bitcast_fusion.2), channel_id=1, source_target_pairs={{0,16},{1,17},{2,18},{3,19},{4,20},{5,21},{6,22},{7,23},{8,24},{9,... | collective-permute-start | bytes 49160 | tf_op jit(solution)/shard_map/ppermute | solution.py:13
  262.2 2.6 copy-start.2
  347.5 3.3 collective-permute-start.9
  349.4 6.8 %collective-permute-start.10 = (f32[16,2,128]{2,0,1:T(8,128)S(1)}, f32[16,2,128]{2,0,1:T(8,128)S(1)}, u32[]{:S(2)}, u32[]{:S(2)}) collective-permute-start(f32[16,2,128]{2,0,1:T(8,128)S(1)} %select_bitcast_fusion.1), channel_id=1, source_target_pairs={{0,1},{1,2},{2,3},{3,4},{4,5},{5,6},{6,7},{7,8},{8,9},{9,10},{10,1... | collective-permute-start | bytes 49160 | tf_op jit(solution)/shard_map/ppermute | solution.py:13
  349.4 6.8 %collective-permute-start.11 = (f32[16,2,128]{2,0,1:T(8,128)S(1)}, f32[16,2,128]{2,0,1:T(8,128)S(1)}, u32[]{:S(2)}, u32[]{:S(2)}) collective-permute-start(f32[16,2,128]{2,0,1:T(8,128)S(1)} %select_bitcast_fusion.1), channel_id=1, source_target_pairs={{0,16},{1,17},{2,18},{3,19},{4,20},{5,21},{6,22},{7,23},{8,24},{9,... | collective-permute-start | bytes 49160 | tf_op jit(solution)/shard_map/ppermute | solution.py:13
  356.8 2.6 copy-start.3
  441.6 3.3 collective-permute-start.12
  443.5 6.9 %collective-permute-start.13 = (f32[16,2,128]{2,0,1:T(8,128)S(1)}, f32[16,2,128]{2,0,1:T(8,128)S(1)}, u32[]{:S(2)}, u32[]{:S(2)}) collective-permute-start(f32[16,2,128]{2,0,1:T(8,128)S(1)} %select_bitcast_fusion), channel_id=1, source_target_pairs={{0,1},{1,2},{2,3},{3,4},{4,5},{5,6},{6,7},{7,8},{8,9},{9,10},{10,1... | collective-permute-start | bytes 49160 | tf_op jit(solution)/shard_map/ppermute | solution.py:13
  443.7 6.8 %collective-permute-start.14 = (f32[16,2,128]{2,0,1:T(8,128)S(1)}, f32[16,2,128]{2,0,1:T(8,128)S(1)}, u32[]{:S(2)}, u32[]{:S(2)}) collective-permute-start(f32[16,2,128]{2,0,1:T(8,128)S(1)} %select_bitcast_fusion), channel_id=1, source_target_pairs={{0,16},{1,17},{2,18},{3,19},{4,20},{5,21},{6,22},{7,23},{8,24},{9,... | collective-permute-start | bytes 49160 | tf_op jit(solution)/shard_map/ppermute | solution.py:13
  451.0 2.6 copy-start.4
where the time goes:
time: 545 us; the launch traced here: 536 us
  blocking collectives  434 us (80%)
  matrix products  36.2 us (7%)
  waiting for transfers between devices  24.7 us (5%)
  local copies, waits for them, and re-layouts  15 us (3%)
  starting transfers between devices  13.8 us (3%)
  other arithmetic  10.7 us (2%)
    psum x4, blocking collectives, shards(): right = lax.psum(product(correct, ortho.T) * scale, 'parts')  163 us
    psum x4, blocking collectives, shards(): left = lax.psum(product(image, test_basis.T) * scale, 'parts')  148 us
    psum x1, blocking collectives, shards(): gram = lax.psum(product(basis, basis.T) * scale, 'parts')  42.1 us
    psum x1, blocking collectives, shards(): final = lax.psum(product(correct, ortho.T) * scale, 'parts')  41 us
    psum x1, blocking collectives, shards(): lax.psum((product(m_ortho, m_ortho.T) * scale, product(m_ortho, k_ortho.T...  40.2 us
    ppermute x15, waiting for transfers between devices, shifted(): return lax.ppermute(value, axis, pairs)  24.7 us
    dot_general x5, matrix products, apply_pair(): jnp.einsum('ptbc,tbrc->ptr', picked, k_tiles, precision=lax.Precision.HIG...  14.9 us
    ppermute x15, starting transfers between devices, shifted(): return lax.ppermute(value, axis, pairs)  13.8 us
  transfers between devices with their start and end apart: 15, of which 7 were waited for; matrix products, arithmetic and copies ran while one was open for 2% of the time, Pallas kernels for 0%

commit v1 on v0

--- a/solution.py
+++ b/solution.py
@@ -72,7 +72,7 @@
         moved = correct - product(right, ortho)
         k_moved, m_moved = apply_pair(moved)
         image = k_moved - theta[:, None] * m_moved
-        left = lax.psum(product(image, test_basis.T) * scale, "parts")
+        left = jnp.sum(lax.all_gather(product(image, test_basis.T) * scale, "parts"), axis=0)
         image = image - product(left, test_basis)
         correct = correct - relax * (resid + image) / diag_k
     final = lax.psum(product(correct, ortho.T) * scale, "parts")

time: 545 us -> 526 us (0.965); the launches traced: 536 us -> 524 us
  blocking collectives: 434 us -> 420 us
  starting transfers between devices: 13.8 us -> 21.3 us
  waiting for transfers between devices: 24.7 us -> 19 us
    all_gather x0 -> x4, blocking collectives: none -> 150 us  [shards(): lax.all_gather(product(image, test_basis.T) * scale, 'parts')]
    psum x4 -> x0, blocking collectives: 148 us -> none  [shards(): left = lax.psum(product(image, test_basis.T) * scale, 'parts')]
    psum x4, blocking collectives: 163 us -> 151 us  [shards(): right = lax.psum(product(correct, ortho.T) * scale, 'parts')]
    ppermute x15, starting transfers between devices: 13.8 us -> 21.3 us  [shifted(): return lax.ppermute(value, axis, pairs)]
    ppermute x15, waiting for transfers between devices: 24.7 us -> 19 us  [shifted(): return lax.ppermute(value, axis, pairs)]
  transfers between devices with their start and end apart: 15 -> 15, of which waited for: 7 -> 4; matrix products, arithmetic and copies ran while one was open for 2% -> 2% of each run, Pallas kernels for 0% -> 0%
where the time goes in v1:
time: 526 us; the launch traced here: 524 us
  blocking collectives  420 us (80%)
  matrix products  36 us (7%)
  starting transfers between devices  21.3 us (4%)
  waiting for transfers between devices  19 us (4%)
  local copies, waits for them, and re-layouts  15.3 us (3%)
  other arithmetic  10.9 us (2%)
    psum x4, blocking collectives, shards(): right = lax.psum(product(correct, ortho.T) * scale, 'parts')  151 us
    all_gather x4, blocking collectives, shards(): lax.all_gather(product(image, test_basis.T) * scale, 'parts')  150 us
    psum x1, blocking collectives, shards(): gram = lax.psum(product(basis, basis.T) * scale, 'parts')  42.1 us
    psum x1, blocking collectives, shards(): lax.psum((product(m_ortho, m_ortho.T) * scale, product(m_ortho, k_ortho.T...  40.2 us
    psum x1, blocking collectives, shards(): final = lax.psum(product(correct, ortho.T) * scale, 'parts')  36.9 us
    ppermute x15, starting transfers between devices, shifted(): return lax.ppermute(value, axis, pairs)  21.3 us
    ppermute x15, waiting for transfers between devices, shifted(): return lax.ppermute(value, axis, pairs)  19 us
    dot_general x5, matrix products, apply_pair(): jnp.einsum('ptbc,tbrc->ptr', picked, k_tiles, precision=lax.Precision.HIG...  14.9 us
  transfers between devices with their start and end apart: 15, of which 4 were waited for; matrix products, arithmetic and copies ran while one was open for 2% of the time, Pallas kernels for 0%

profile of v1, /device:TPU:0, one launch (start us, length us, event | category | flops | bytes accessed | tf_op | source)
XLA Modules:
  0.0 524.1 jit_solution(6854986814906240511)
XLA Ops:
  0.6 0.8 compare_select_fusion.1
  2.1 1.1 convolution_multiply_fusion.9
  3.2 42.1 %psum.56 = f32[16,16]{0,1:T(8,128)S(1)} all-reduce(f32[16,16]{0,1:T(8,128)S(1)} %convolution_multiply_fusion.9), channel_id=1, replica_groups=mesh['parts'=32] {'parts'}, use_global_device_ids=true, to_apply=%region_0.1 | all-reduce | flops 256 | bytes 2048 | tf_op jit(solution)/shard_map/psum | solution.py:55
  45.3 1.5 cholesky.44
  48.1 1.2 custom-call.12
  49.6 1.0 fusion.99
  51.3 2.5 collective-permute-start
  53.8 0.8 collective-permute-start.2
  54.6 0.7 compare_and_fusion
  55.4 1.1 slice.11
  56.5 4.6 copy.136
  61.1 1.8 gather_fusion.2
  63.6 4.3 fusion.32
  68.0 2.6 fusion.30
  71.0 40.2 %all-reduce = (f32[16,16]{0,1:T(8,128)S(1)}, f32[16,16]{0,1:T(8,128)S(1)}) all-reduce(f32[16,16]{0,1:T(8,128)S(1)} %fusion.21, f32[16,16]{0,1:T(8,128)S(1)} %fusion.20), channel_id=1, replica_groups=mesh['parts'=32] {'parts'}, use_global_device_ids=true, to_apply=%region_3.8 | all-reduce | flops 512 | bytes 4096 | tf_op jit(solution)/shard_map/psum | solution.py:59
  111.3 1.5 cholesky.55
  114.1 1.2 custom-call.13
  115.9 0.7 gather_fusion
  117.5 39.9 %psum.59 = f32[16,16]{0,1:T(8,128)S(1)} all-reduce(f32[16,16]{0,1:T(8,128)S(1)} %convolution_multiply_fusion.8), channel_id=1, replica_groups=mesh['parts'=32] {'parts'}, use_global_device_ids=true, to_apply=%region_5.10 | all-reduce | flops 256 | bytes 2048 | tf_op jit(solution)/shard_map/psum | solution.py:71
  158.3 2.2 collective-permute-start.3
  160.5 1.8 collective-permute-start.5
  162.3 5.0 collective-permute-done.4
  167.9 2.6 convolution_bitcast_fusion.6
  170.5 2.7 convolution_bitcast_fusion.7
  173.5 37.1 %all-gather = f32[512,16]{1,0:T(8,128)S(1)} all-gather(f32[16,16]{1,0:T(8,128)S(1)} %copy.77), channel_id=2, replica_groups=mesh['parts'=32] {'parts'}, dimensions={0}, use_global_device_ids=true | all-gather | bytes 33792 | tf_op jit(solution)/shard_map/all_gather | solution.py:75
  211.0 37.3 %psum.60 = f32[16,16]{0,1:T(8,128)S(1)} all-reduce(f32[16,16]{0,1:T(8,128)S(1)} %convolution_multiply_fusion.6), channel_id=1, replica_groups=mesh['parts'=32] {'parts'}, use_global_device_ids=true, to_apply=%region_7.12 | all-reduce | flops 256 | bytes 2048 | tf_op jit(solution)/shard_map/psum | solution.py:71
  249.2 2.6 collective-permute-start.6
  251.8 2.0 collective-permute-start.8
  253.8 4.7 collective-permute-done.7
  259.2 2.6 convolution_bitcast_fusion.4
  261.8 2.7 convolution_bitcast_fusion.5
  264.9 37.8 %all-gather.1 = f32[512,16]{1,0:T(8,128)S(1)} all-gather(f32[16,16]{1,0:T(8,128)S(1)} %copy.85), channel_id=3, replica_groups=mesh['parts'=32] {'parts'}, dimensions={0}, use_global_device_ids=true | all-gather | bytes 33792 | tf_op jit(solution)/shard_map/all_gather | solution.py:75
  303.1 37.1 %psum.61 = f32[16,16]{0,1:T(8,128)S(1)} all-reduce(f32[16,16]{0,1:T(8,128)S(1)} %convolution_multiply_fusion.4), channel_id=1, replica_groups=mesh['parts'=32] {'parts'}, use_global_device_ids=true, to_apply=%region_9.14 | all-reduce | flops 256 | bytes 2048 | tf_op jit(solution)/shard_map/psum | solution.py:71
  341.1 2.6 collective-permute-start.9
  343.7 2.1 collective-permute-start.11
  345.9 4.6 collective-permute-done.10
  351.1 2.6 convolution_bitcast_fusion.2
  353.8 2.7 convolution_bitcast_fusion.3
  356.8 37.5 %all-gather.2 = f32[512,16]{1,0:T(8,128)S(1)} all-gather(f32[16,16]{1,0:T(8,128)S(1)} %copy.93), channel_id=4, replica_groups=mesh['parts'=32] {'parts'}, dimensions={0}, use_global_device_ids=true | all-gather | bytes 33792 | tf_op jit(solution)/shard_map/all_gather | solution.py:75
  394.7 36.9 %psum.62 = f32[16,16]{0,1:T(8,128)S(1)} all-reduce(f32[16,16]{0,1:T(8,128)S(1)} %convolution_multiply_fusion.2), channel_id=1, replica_groups=mesh['parts'=32] {'parts'}, use_global_device_ids=true, to_apply=%region_11.16 | all-reduce | flops 256 | bytes 2048 | tf_op jit(solution)/shard_map/psum | solution.py:71
  432.5 2.6 collective-permute-start.12
  435.1 2.1 collective-permute-start.14
  437.2 4.6 collective-permute-done.13
  442.5 2.6 convolution_bitcast_fusion
  445.1 2.7 convolution_bitcast_fusion.1
  448.2 37.8 %all-gather.3 = f32[512,16]{1,0:T(8,128)S(1)} all-gather(f32[16,16]{1,0:T(8,128)S(1)} %copy.101), channel_id=5, replica_groups=mesh['parts'=32] {'parts'}, dimensions={0}, use_global_device_ids=true | all-gather | bytes 33792 | tf_op jit(solution)/shard_map/all_gather | solution.py:75
  486.4 36.9 %psum.63 = f32[16,16]{0,1:T(8,128)S(1)} all-reduce(f32[16,16]{0,1:T(8,128)S(1)} %convolution_multiply_fusion), channel_id=1, replica_groups=mesh['parts'=32] {'parts'}, use_global_device_ids=true, to_apply=%region_13.18 | all-reduce | flops 256 | bytes 2048 | tf_op jit(solution)/shard_map/psum | solution.py:78
  523.2 0.9 convolution_subtract_fusion
  (124 shorter events, 16.2 us)
Async XLA Ops:
  0.6 67.3 %copy-start = (f32[8,5,128,128]{3,2,1,0:T(8,128)S(1)}, f32[8,5,128,128]{3,2,1,0:T(8,128)}, u32[]{:S(2)}) copy-start(f32[8,5,128,128]{3,2,1,0:T(8,128)} %param.15) | copy-start | bytes 7864324
  51.3 11.7 %collective-permute-start = (f32[16,2,128]{2,0,1:T(8,128)S(1)}, f32[16,2,128]{2,0,1:T(8,128)S(1)}, u32[]{:S(2)}, u32[]{:S(2)}) collective-permute-start(f32[16,2,128]{2,0,1:T(8,128)S(1)} %select_bitcast_fusion.4), channel_id=1, source_target_pairs={{0,31},{1,0},{2,1},{3,2},{4,3},{5,4},{6,5},{7,6},{8,7},{9,8},{10,9... | collective-permute-start | bytes 49160 | tf_op jit(solution)/shard_map/ppermute | solution.py:13
  53.8 9.2 %collective-permute-start.1 = (f32[16,2,128]{2,0,1:T(8,128)S(1)}, f32[16,2,128]{2,0,1:T(8,128)S(1)}, u32[]{:S(2)}, u32[]{:S(2)}) collective-permute-start(f32[16,2,128]{2,0,1:T(8,128)S(1)} %select_bitcast_fusion.4), channel_id=1, source_target_pairs={{0,1},{1,2},{2,3},{3,4},{4,5},{5,6},{6,7},{7,8},{8,9},{9,10},{10,1... | collective-permute-start | bytes 49160 | tf_op jit(solution)/shard_map/ppermute | solution.py:13
  53.8 9.2 %collective-permute-start.2 = (f32[16,2,128]{2,0,1:T(8,128)S(1)}, f32[16,2,128]{2,0,1:T(8,128)S(1)}, u32[]{:S(2)}, u32[]{:S(2)}) collective-permute-start(f32[16,2,128]{2,0,1:T(8,128)S(1)} %select_bitcast_fusion.4), channel_id=1, source_target_pairs={{0,16},{1,17},{2,18},{3,19},{4,20},{5,21},{6,22},{7,23},{8,24},{9,... | collective-permute-start | bytes 49160 | tf_op jit(solution)/shard_map/ppermute | solution.py:13
  117.3 368.7 %copy-start.5 = (f32[16]{0:T(128)}, f32[16]{0:T(128)S(1)}, u32[]{:S(2)}) copy-start(f32[16]{0:T(128)S(1)} %div.47) | copy-start | bytes 196
  158.3 4.0 collective-permute-start.3
  160.5 6.8 %collective-permute-start.4 = (f32[16,2,128]{2,0,1:T(8,128)S(1)}, f32[16,2,128]{2,0,1:T(8,128)S(1)}, u32[]{:S(2)}, u32[]{:S(2)}) collective-permute-start(f32[16,2,128]{2,0,1:T(8,128)S(1)} %select_bitcast_fusion.3), channel_id=1, source_target_pairs={{0,1},{1,2},{2,3},{3,4},{4,5},{5,6},{6,7},{7,8},{8,9},{9,10},{10,1... | collective-permute-start | bytes 49160 | tf_op jit(solution)/shard_map/ppermute | solution.py:13
  160.5 6.8 %collective-permute-start.5 = (f32[16,2,128]{2,0,1:T(8,128)S(1)}, f32[16,2,128]{2,0,1:T(8,128)S(1)}, u32[]{:S(2)}, u32[]{:S(2)}) collective-permute-start(f32[16,2,128]{2,0,1:T(8,128)S(1)} %select_bitcast_fusion.3), channel_id=1, source_target_pairs={{0,16},{1,17},{2,18},{3,19},{4,20},{5,21},{6,22},{7,23},{8,24},{9,... | collective-permute-start | bytes 49160 | tf_op jit(solution)/shard_map/ppermute | solution.py:13
  167.9 2.6 copy-start.1
  249.2 4.6 collective-permute-start.6
  251.8 6.8 %collective-permute-start.7 = (f32[16,2,128]{2,0,1:T(8,128)S(1)}, f32[16,2,128]{2,0,1:T(8,128)S(1)}, u32[]{:S(2)}, u32[]{:S(2)}) collective-permute-start(f32[16,2,128]{2,0,1:T(8,128)S(1)} %select_bitcast_fusion.2), channel_id=1, source_target_pairs={{0,1},{1,2},{2,3},{3,4},{4,5},{5,6},{6,7},{7,8},{8,9},{9,10},{10,1... | collective-permute-start | bytes 49160 | tf_op jit(solution)/shard_map/ppermute | solution.py:13
  251.8 6.8 %collective-permute-start.8 = (f32[16,2,128]{2,0,1:T(8,128)S(1)}, f32[16,2,128]{2,0,1:T(8,128)S(1)}, u32[]{:S(2)}, u32[]{:S(2)}) collective-permute-start(f32[16,2,128]{2,0,1:T(8,128)S(1)} %select_bitcast_fusion.2), channel_id=1, source_target_pairs={{0,16},{1,17},{2,18},{3,19},{4,20},{5,21},{6,22},{7,23},{8,24},{9,... | collective-permute-start | bytes 49160 | tf_op jit(solution)/shard_map/ppermute | solution.py:13
  259.2 2.6 copy-start.2
  341.1 4.7 collective-permute-start.9
  343.7 6.8 %collective-permute-start.10 = (f32[16,2,128]{2,0,1:T(8,128)S(1)}, f32[16,2,128]{2,0,1:T(8,128)S(1)}, u32[]{:S(2)}, u32[]{:S(2)}) collective-permute-start(f32[16,2,128]{2,0,1:T(8,128)S(1)} %select_bitcast_fusion.1), channel_id=1, source_target_pairs={{0,1},{1,2},{2,3},{3,4},{4,5},{5,6},{6,7},{7,8},{8,9},{9,10},{10,1... | collective-permute-start | bytes 49160 | tf_op jit(solution)/shard_map/ppermute | solution.py:13
  343.7 6.8 %collective-permute-start.11 = (f32[16,2,128]{2,0,1:T(8,128)S(1)}, f32[16,2,128]{2,0,1:T(8,128)S(1)}, u32[]{:S(2)}, u32[]{:S(2)}) collective-permute-start(f32[16,2,128]{2,0,1:T(8,128)S(1)} %select_bitcast_fusion.1), channel_id=1, source_target_pairs={{0,16},{1,17},{2,18},{3,19},{4,20},{5,21},{6,22},{7,23},{8,24},{9,... | collective-permute-start | bytes 49160 | tf_op jit(solution)/shard_map/ppermute | solution.py:13
  351.1 2.6 copy-start.3
  432.5 4.7 collective-permute-start.12
  435.1 6.8 %collective-permute-start.13 = (f32[16,2,128]{2,0,1:T(8,128)S(1)}, f32[16,2,128]{2,0,1:T(8,128)S(1)}, u32[]{:S(2)}, u32[]{:S(2)}) collective-permute-start(f32[16,2,128]{2,0,1:T(8,128)S(1)} %select_bitcast_fusion), channel_id=1, source_target_pairs={{0,1},{1,2},{2,3},{3,4},{4,5},{5,6},{6,7},{7,8},{8,9},{9,10},{10,1... | collective-permute-start | bytes 49160 | tf_op jit(solution)/shard_map/ppermute | solution.py:13
  435.1 6.8 %collective-permute-start.14 = (f32[16,2,128]{2,0,1:T(8,128)S(1)}, f32[16,2,128]{2,0,1:T(8,128)S(1)}, u32[]{:S(2)}, u32[]{:S(2)}) collective-permute-start(f32[16,2,128]{2,0,1:T(8,128)S(1)} %select_bitcast_fusion), channel_id=1, source_target_pairs={{0,16},{1,17},{2,18},{3,19},{4,20},{5,21},{6,22},{7,23},{8,24},{9,... | collective-permute-start | bytes 49160 | tf_op jit(solution)/shard_map/ppermute | solution.py:13
  442.5 2.6 copy-start.4
